TPU v7x, 32 devices: a whole 2x2x4 slice. The times are simulated.
32 devices in a mesh: seq: 4 (over y, x), batch: 8 (over z, core).
Axes of the slice: x: 2, y: 2, z: 4, core: 2. Of those that a mesh axis runs over, the one named last changes fastest.
Arguments:
- tokens: bfloat16 [8, 1024, 2048], P('batch', 'seq'), may hold values from -6 to 6
- cotangent: bfloat16 [8, 1024, 2048], P('batch', 'seq'), may hold values from -6 to 6
- segment_ids: int32 [8, 1024], P('batch'), may hold values from 0 to 4, as said below
- positions: int32 [8, 1024], P('batch'), may hold values from 0 to 511, as said below
- attn_gain: float32 [2048], replicated, may hold values from 0.5 to 1.5
- qkv_weight: bfloat16 [2048, 2560], P('batch'), may hold values from -0.125 to 0.125
- out_weight: bfloat16 [2048, 2048], P('batch'), may hold values from -0.75 to 0.75
- mlp_gain: float32 [2048], replicated, may hold values from 0.5 to 1.5
- gate_up_weight: bfloat16 [2048, 11264], P('batch'), may hold values from -0.125 to 0.125
- down_weight: bfloat16 [5632, 2048], P('batch'), may hold values from -0.078125 to 0.078125
Outputs:
- output: bfloat16 [8, 1024, 2048], P('batch', 'seq')
- tokens_grad: bfloat16 [8, 1024, 2048], P('batch', 'seq')
- attn_gain_grad: float32 [2048], replicated
- qkv_weight_grad: float32 [2048, 2560], P('batch')
- out_weight_grad: float32 [2048, 2048], P('batch')
- mlp_gain_grad: float32 [2048], replicated
- gate_up_weight_grad: float32 [2048, 11264], P('batch')
- down_weight_grad: float32 [5632, 2048], P('batch')
Inputs may be any that keep to these rules, and one draw needn't show every extreme that they name: `segment_ids`: within each packed sequence the ids start at 0, rise by one at each new document and never fall; a document has 1 to 512 tokens and never crosses a multiple of 512 tokens; every sequence holds one document of exactly 512 tokens and 5 documents in all. `positions`: A token's position within its document: 0 at the document's first token, rising by one per token; consistent with segment_ids.
All inputs are finite; a program needn't handle non-finite values.
Results may differ from a plain program's by a relative error of at most 0.02.
Values may be sent and summed in bfloat16 or wider, within the bound.
A program may use at most 384 MiB of HBM per device.

v0:
```python
import jax
import jax.numpy as jnp
from jax import lax
from jax.sharding import PartitionSpec as P

H = 32
KV = 4
HD = 64
BLOCK_ROWS = 512


def rms_parts(values, gain_vector):
    inv_rms = lax.rsqrt(jnp.mean(values * values, axis=-1, keepdims=True) + 1e-05)
    return (values * inv_rms * gain_vector, inv_rms)


def norm_back(grad_normed, values, inv_rms, gain_vector):
    weighted = grad_normed * gain_vector
    inner_sum = jnp.mean(weighted * values, axis=-1, keepdims=True)
    return inv_rms * weighted - values * (inv_rms * inv_rms * inv_rms) * inner_sum


def rotary_tables(seq_positions, head_dim):
    half_dim = head_dim // 2
    frequency = 10000.0 ** (-jnp.arange(half_dim, dtype=jnp.float32) * 2.0 / head_dim)
    angles = seq_positions.astype(jnp.float32)[:, None] * frequency[None, :]
    return (jnp.cos(angles)[:, None, :], jnp.sin(angles)[:, None, :])


def rotate(values, cosine, sine_part):
    half_dim = values.shape[-1] // 2
    first_half = values[..., :half_dim]
    second_half = values[..., half_dim:]
    return jnp.concatenate(
        [
            first_half * cosine - second_half * sine_part,
            second_half * cosine + first_half * sine_part,
        ],
        axis=-1,
    )


def fold_product(inputs, weight):
    return jnp.dot(
        inputs,
        lax.all_gather(weight, "batch", axis=0, tiled=True),
        preferred_element_type=jnp.float32,
    )


def transposed_product(grads_out, weight):
    return lax.dot_general(
        grads_out,
        lax.all_gather(weight, "batch", axis=0, tiled=True),
        (((1,), (1,)), ((), ())),
        preferred_element_type=jnp.float32,
    )


def weight_gradient(inputs, grads_out):
    return lax.psum_scatter(
        lax.dot_general(
            inputs, grads_out, (((0,), (0,)), ((), ())), preferred_element_type=jnp.float32
        ).astype(jnp.bfloat16),
        "batch",
        scatter_dimension=0,
        tiled=True,
    ).astype(jnp.float32)


def column_heads(values):
    return lax.all_to_all(values, "seq", split_axis=1, concat_axis=0, tiled=True)


def local(
    tokens,
    cotangent,
    segment_ids,
    positions,
    attn_gain,
    qkv_weight,
    out_weight,
    mlp_gain,
    gate_up_weight,
    down_weight,
):
    seq_count = lax.axis_size("seq")
    model_width = tokens.shape[2]
    local_rows = tokens.shape[1]
    seq_len = local_rows * seq_count
    heads_local = H // seq_count
    groups_all = max(KV, seq_count)
    kv_local = groups_all // seq_count
    copies_each = groups_all // KV
    group_share = heads_local // kv_local
    block_total = seq_len // BLOCK_ROWS
    scale_factor = HD ** (-0.5)
    inputs = tokens[0].astype(jnp.float32)
    normed, inv_first = rms_parts(inputs, attn_gain)
    normed_low = normed.astype(jnp.bfloat16)
    projected = fold_product(normed_low, qkv_weight)
    queries_low = projected[:, :model_width].astype(jnp.bfloat16)
    key_cols = projected[:, model_width : model_width + KV * HD].reshape(local_rows, KV, HD)
    value_cols = projected[:, model_width + KV * HD :].reshape(local_rows, KV, HD)
    keys_dup = (
        jnp.repeat(key_cols, copies_each, axis=1)
        .reshape(local_rows, groups_all * HD)
        .astype(jnp.bfloat16)
    )
    values_dup = (
        jnp.repeat(value_cols, copies_each, axis=1)
        .reshape(local_rows, groups_all * HD)
        .astype(jnp.bfloat16)
    )
    head_queries, head_keys, head_values = (
        lax.all_to_all(queries_low, "seq", split_axis=1, concat_axis=0, tiled=True),
        lax.all_to_all(keys_dup, "seq", split_axis=1, concat_axis=0, tiled=True),
        lax.all_to_all(values_dup, "seq", split_axis=1, concat_axis=0, tiled=True),
    )
    seq_segments = segment_ids[0]
    cosine, sine_part = rotary_tables(positions[0], HD)
    queries_rot = rotate(
        head_queries.reshape(seq_len, heads_local, HD).astype(jnp.float32), cosine, sine_part
    )
    queries_rot = queries_rot.astype(jnp.bfloat16).reshape(seq_len, kv_local, group_share, HD)
    keys_rot = rotate(
        head_keys.reshape(seq_len, kv_local, HD).astype(jnp.float32), cosine, sine_part
    ).astype(jnp.bfloat16)
    values_heads = head_values.reshape(seq_len, kv_local, HD)
    token_index = jnp.arange(seq_len, dtype=jnp.int32)

    def block_scores(block_index, query_block):
        row_start = block_index * BLOCK_ROWS
        query_ids = lax.dynamic_slice_in_dim(token_index, row_start, BLOCK_ROWS, 0)
        query_segments = lax.dynamic_slice_in_dim(seq_segments, row_start, BLOCK_ROWS, 0)
        allowed = (token_index[None, :] <= query_ids[:, None]) & (
            seq_segments[None, :] == query_segments[:, None]
        )
        scores = (
            jnp.einsum("qgsd,kgd->gsqk", query_block, keys_rot, preferred_element_type=jnp.float32)
            * scale_factor
        )
        return jnp.where(allowed[None, None], scores, -1e30)

    def attend(block_index):
        query_block = lax.dynamic_slice_in_dim(queries_rot, block_index * BLOCK_ROWS, BLOCK_ROWS, 0)
        masked = block_scores(block_index, query_block)
        row_max = jnp.max(masked, axis=-1, keepdims=True)
        log_total = row_max + jnp.log(jnp.sum(jnp.exp(masked - row_max), axis=-1, keepdims=True))
        probs_low = jnp.exp(masked - log_total).astype(jnp.bfloat16)
        attended = jnp.einsum(
            "gsqk,kgd->qgsd", probs_low, values_heads, preferred_element_type=jnp.float32
        )
        return (attended.astype(jnp.bfloat16), log_total[..., 0])

    attended_all, log_totals = lax.map(attend, jnp.arange(block_total, dtype=jnp.int32))
    attended_all = attended_all.reshape(seq_len, heads_local * HD)
    attn_tokens = lax.all_to_all(attended_all, "seq", split_axis=0, concat_axis=1, tiled=True)
    attn_proj = fold_product(attn_tokens, out_weight)
    residual = inputs + attn_proj
    normed_mlp, inv_second = rms_parts(residual, mlp_gain)
    normed_mlp_low = normed_mlp.astype(jnp.bfloat16)
    gate_up = fold_product(normed_mlp_low, gate_up_weight)
    ff_width = gate_up.shape[1] // 2
    gate_part = gate_up[:, :ff_width]
    up_part = gate_up[:, ff_width:]
    sigmoid_gate = jax.nn.sigmoid(gate_part)
    hidden_low = (gate_part * sigmoid_gate * up_part).astype(jnp.bfloat16)
    down_out = fold_product(hidden_low, down_weight)
    output = (residual + down_out).astype(jnp.bfloat16)
    grad_out = cotangent[0].astype(jnp.float32)
    grad_down = grad_out.astype(jnp.bfloat16)
    down_part = weight_gradient(hidden_low, grad_down)
    grad_hidden = transposed_product(grad_down, down_weight)
    grad_gate = grad_hidden * up_part * sigmoid_gate * (1.0 + gate_part * (1.0 - sigmoid_gate))
    grad_up = grad_hidden * gate_part * sigmoid_gate
    grad_gate_up = jnp.concatenate([grad_gate, grad_up], axis=1).astype(jnp.bfloat16)
    gate_up_part = weight_gradient(normed_mlp_low, grad_gate_up)
    grad_normed_mlp = transposed_product(grad_gate_up, gate_up_weight)
    mlp_term = jnp.sum(grad_normed_mlp * residual * inv_second, axis=0)
    grad_resid = grad_out + norm_back(grad_normed_mlp, residual, inv_second, mlp_gain)
    grad_proj = grad_resid.astype(jnp.bfloat16)
    out_part = weight_gradient(attn_tokens, grad_proj)
    grad_attn = transposed_product(grad_proj, out_weight).astype(jnp.bfloat16)
    grad_heads = column_heads(grad_attn)
    grad_heads = grad_heads.reshape(seq_len, kv_local, group_share, HD)

    def attend_back(carried, inputs_block):
        key_acc, value_acc = carried
        block_index, log_total = inputs_block
        query_block = lax.dynamic_slice_in_dim(queries_rot, block_index * BLOCK_ROWS, BLOCK_ROWS, 0)
        grad_block = lax.dynamic_slice_in_dim(grad_heads, block_index * BLOCK_ROWS, BLOCK_ROWS, 0)
        masked = block_scores(block_index, query_block)
        softmax_rows = jnp.exp(masked - log_total[..., None])
        probs_low = softmax_rows.astype(jnp.bfloat16)
        grad_probs = jnp.einsum(
            "qgsd,kgd->gsqk", grad_block, values_heads, preferred_element_type=jnp.float32
        )
        inner_sum = jnp.sum(softmax_rows * grad_probs, axis=-1, keepdims=True)
        grad_scores = (softmax_rows * (grad_probs - inner_sum)).astype(jnp.bfloat16)
        grad_query = (
            jnp.einsum("gsqk,kgd->qgsd", grad_scores, keys_rot, preferred_element_type=jnp.float32)
            * scale_factor
        )
        key_acc = (
            key_acc
            + jnp.einsum(
                "gsqk,qgsd->kgd", grad_scores, query_block, preferred_element_type=jnp.float32
            )
            * scale_factor
        )
        value_acc = value_acc + jnp.einsum(
            "gsqk,qgsd->kgd", probs_low, grad_block, preferred_element_type=jnp.float32
        )
        return ((key_acc, value_acc), grad_query)

    empty_heads = jnp.zeros((seq_len, kv_local, HD), jnp.float32)
    (grad_keys, grad_values), grad_queries = lax.scan(
        attend_back,
        (empty_heads, empty_heads),
        (jnp.arange(block_total, dtype=jnp.int32), log_totals),
    )
    grad_queries = grad_queries.reshape(seq_len, heads_local, HD)
    back_queries = (
        rotate(grad_queries, cosine, -sine_part)
        .reshape(seq_len, heads_local * HD)
        .astype(jnp.bfloat16)
    )
    back_keys = (
        rotate(grad_keys, cosine, -sine_part).reshape(seq_len, kv_local * HD).astype(jnp.bfloat16)
    )
    back_values = grad_values.reshape(seq_len, kv_local * HD).astype(jnp.bfloat16)
    token_queries, token_keys, token_values = (
        lax.all_to_all(back_queries, "seq", split_axis=0, concat_axis=1, tiled=True),
        lax.all_to_all(back_keys, "seq", split_axis=0, concat_axis=1, tiled=True),
        lax.all_to_all(back_values, "seq", split_axis=0, concat_axis=1, tiled=True),
    )
    key_sum = token_keys.astype(jnp.float32).reshape(local_rows, KV, copies_each, HD).sum(axis=2)
    value_sum = (
        token_values.astype(jnp.float32).reshape(local_rows, KV, copies_each, HD).sum(axis=2)
    )
    grad_qkv = jnp.concatenate(
        [
            token_queries,
            key_sum.reshape(local_rows, KV * HD).astype(jnp.bfloat16),
            value_sum.reshape(local_rows, KV * HD).astype(jnp.bfloat16),
        ],
        axis=1,
    )
    qkv_part = weight_gradient(normed_low, grad_qkv)
    grad_normed = transposed_product(grad_qkv, qkv_weight)
    attn_term = jnp.sum(grad_normed * inputs * inv_first, axis=0)
    tokens_grad = (grad_resid + norm_back(grad_normed, inputs, inv_first, attn_gain)).astype(
        jnp.bfloat16
    )
    attn_gain_grad, mlp_gain_grad = lax.psum((attn_term, mlp_term), ("seq", "batch"))
    qkv_grad, out_grad, gate_up_grad, down_grad = (
        lax.psum(qkv_part.astype(jnp.bfloat16), "seq").astype(jnp.float32),
        lax.psum(out_part.astype(jnp.bfloat16), "seq").astype(jnp.float32),
        lax.psum(gate_up_part.astype(jnp.bfloat16), "seq").astype(jnp.float32),
        lax.psum(down_part.astype(jnp.bfloat16), "seq").astype(jnp.float32),
    )
    return (
        output[None],
        tokens_grad[None],
        attn_gain_grad,
        qkv_grad,
        out_grad,
        mlp_gain_grad,
        gate_up_grad,
        down_grad,
    )


def solution(mesh):
    return jax.shard_map(
        local,
        mesh=mesh,
        in_specs=(
            P("batch", "seq", None),
            P("batch", "seq", None),
            P("batch", None),
            P("batch", None),
            P(),
            P("batch", None),
            P("batch", None),
            P(),
            P("batch", None),
            P("batch", None),
        ),
        out_specs=(
            P("batch", "seq", None),
            P("batch", "seq", None),
            P(),
            P("batch", None),
            P("batch", None),
            P(),
            P("batch", None),
            P("batch", None),
        ),
        check_vma=False,
    )
```

profile of v0, /device:TPU:0, one launch (start us, length us, event | category | flops | bytes accessed | tf_op | source)
XLA Modules:
  0.0 2058.5 jit_solution(16051898842681383244)
XLA Ops:
  10.8 100.9 %all-gather.5.cloned.1.call-done = bf16[2048,2560]{1,0:T(8,128)(2,1)} async-done(((bf16[256,2560]{1,0:T(8,128)(2,1)}), bf16[2048,2560]{1,0:T(8,128)(2,1)}) %all-gather.5.cloned.1.call-update) | async-done | bytes 10485776 | tf_op jit(solution)/shard_map/all_gather | solution.py:46
  111.8 6.9 convolution_convert_fusion.4
  144.6 8.7 all-to-all-done
  159.6 31.4 %while.29 = (s32[]{:T(128)}, bf16[2,512,1,8,64]{1,4,3,2,0:T(8,128)(2,1)}, f32[2,1,8,512]{3,2,1,0:T(8,128)}, s32[1024]{0:T(1024)S(1)}, s32[2]{0:T(128)S(1)}, /*in...) while((s32[]{:T(128)}, ...), condition=%wide.region_4.5_spmd.clone, body=%wide.region_1.4_spmd.clone.sunk | while | flops 1121710080 | bytes 63066468 | solution.py:156
  201.0 12.5 all-to-all-done.3
  213.6 8.2 multiply_reduce_fusion.2
  221.8 365.3 %all-gather.9.cloned.1.call-done = bf16[2048,11264]{1,0:T(8,128)(2,1)} async-done(((bf16[256,11264]{1,0:T(8,128)(2,1)}), bf16[2048,11264]{1,0:T(8,128)(2,1)}) %all-gather.9.cloned.1.call-update) | async-done | bytes 46137360 | tf_op jit(solution)/shard_map/all_gather | solution.py:46
  587.1 25.8 %fusion.103 = f32[256,11264]{1,0:T(8,128)} fusion(bf16[2048,11264]{1,0:T(8,128)(2,1)} %all-gather.9.cloned.1.call-done, f32[256,2048]{1,0:T(8,128)} %get-tuple-element.333, f32[2048]{0:T(1024)S(1)} %copy-done.25, f32[256]{0:T(256)S(1)} %get-tuple-element.331), kind=kOutput, calls=%fused_computation.150 | convolution fusion | flops 11812732928 | bytes 59778048 | tf_op jit(solution)/shard_map/dot_general | solution.py:44
  612.9 176.7 %all-gather.11.cloned.1.call-done = bf16[5632,2048]{1,0:T(8,128)(2,1)} async-done(((bf16[704,2048]{1,0:T(8,128)(2,1)}), bf16[5632,2048]{1,0:T(8,128)(2,1)}) %all-gather.11.cloned.1.call-update) | async-done | bytes 23068688 | tf_op jit(solution)/shard_map/all_gather | solution.py:46
  789.6 18.5 multiply_convert_fusion.1
  808.1 22.1 %multiply_reduce_fusion = (f32[2048]{0:T(1024)}, f32[256]{0:T(256)S(1)}, f32[256,2048]{1,0:T(8,128)}) fusion(f32[256,2048]{1,0:T(8,128)S(1)} %copy-done.3, f32[256]{0:T(256)S(1)} %get-tuple-element.331, f32[2048]{0:T(1024)S(1)} %copy-done.25, bf16[2048,11264]{1,0:T(8,128)(2,1)} %all-gather.9.cloned.1.call-done, bf16[256,5632]{1,0:T(8,128)(2,1)} %get-tuple-element.313, ...), kind=kOutput, calls=%fused_computation.91 | convolution fusion | flops 11825838080 | bytes 56117248 | tf_op jit(solution)/shard_map/dot_general | solution.py:52
  852.4 14.2 all-to-all-done.4
  868.8 128.6 %while.30 = (s32[]{:T(128)}, f32[1024,1,64]{0,2,1:T(8,128)}, f32[1024,1,64]{0,2,1:T(8,128)}, f32[2,512,1,8,64]{1,0,4,3,2:T(2,128)}, s32[2]{0:T(128)S(1)}, /*inde...) while((s32[]{:T(128)}, f32[1024,1,64]{0,2,1:T(8,128)}, ...), condition=%wide.region_9.10_spmd.clone.clone, body=%wide.region_7.9_spmd.clone.clone.sunk | while | flops 2724261888 | bytes 167350704 | solution.py:218
  875.6 10.4 fusion.150
  886.0 9.3 fusion.151
  901.2 7.7 fusion.153
  913.7 19.5 dynamic_update_slice.23
  940.0 10.4 fusion.150
  950.4 9.3 fusion.151
  965.6 7.6 fusion.153
  977.9 19.5 dynamic_update_slice.23
  1018.4 14.8 all_to_all.125
  1034.1 6.8 convolution_convert_fusion.2
  1042.2 13.2 convolution_convert_fusion.1
  1057.0 21.3 %convolution_convert_fusion = bf16[2048,11264]{1,0:T(8,128)(2,1)} fusion(bf16[256,5632]{1,0:T(8,128)(2,1)} %get-tuple-element.313, bf16[256,5632]{1,0:T(8,128)(2,1)} %get-tuple-element.312, f32[256,2048]{1,0:T(8,128)S(1)} %copy-done.4, f32[2048]{0:T(1024)S(1)} %copy-done.26, f32[256]{0:T(256)S(1)} %copy-done.28), kind=kOutput, calls=%fused_computation.59 | convolution fusion | flops 11847335936 | bytes 54010880 | tf_op jit(solution)/shard_map/dot_general | solution.py:62
  1078.4 68.7 %reduce-scatter.7.cloned.1.call-done = bf16[256,2560]{1,0:T(8,128)(2,1)} async-done(((bf16[2048,2560]{1,0:T(8,128)(2,1)}), bf16[256,2560]{1,0:T(8,128)(2,1)}) %reduce-scatter.7.cloned.1.call-update) | async-done | bytes 1310736 | tf_op jit(solution)/shard_map/reduce_scatter | solution.py:61
  1147.1 228.2 %reduce-scatter.11.cloned.1.call-done = bf16[704,2048]{1,0:T(8,128)(2,1)} async-done(((bf16[5632,2048]{1,0:T(8,128)(2,1)}), bf16[704,2048]{1,0:T(8,128)(2,1)}) %reduce-scatter.11.cloned.1.call-update) | async-done | bytes 2883600 | tf_op jit(solution)/shard_map/reduce_scatter | solution.py:61
  1375.4 444.5 %reduce-scatter.13.cloned.1.call-done = bf16[256,11264]{1,0:T(8,128)(2,1)} async-done(((bf16[2048,11264]{1,0:T(8,128)(2,1)}), bf16[256,11264]{1,0:T(8,128)(2,1)}) %reduce-scatter.13.cloned.1.call-update) | async-done | bytes 5767184
  1819.9 13.5 fusion.59
  1833.4 9.1 fusion.69
  1842.5 38.8 %all-reduce.1 = (f32[2048]{0:T(1024)}, f32[2048]{0:T(1024)}) all-reduce(f32[2048]{0:T(1024)S(1)} %get-tuple-element.252, f32[2048]{0:T(1024)S(1)} %copy-done.38), channel_id=1, replica_groups=mesh['seq'=4,'batch'=8] {'seq','batch'}, use_global_device_ids=true, to_apply=%region_12.13 | all-reduce | flops 4096 | bytes 32768 | tf_op jit(solution)/shard_map/psum | solution.py:256
  1884.5 153.3 %all-reduce.5.cloned.1.call-done = (bf16[256,2560]{1,0:T(8,128)(2,1)}, bf16[256,2048]{1,0:T(8,128)(2,1)}, bf16[256,11264]{1,0:T(8,128)(2,1)}, bf16[704,2048]{1,0:T(8,128)(2,1)}) async-done(((bf16[256,2560]{1,0:T(8,128)(2,1)}, bf16[256,2048]{1,0:T(8,128)(2,1)}, bf16[256,11264]{1,0:T(8,128)(2,1)}, bf16[704,2048]{1,0:T(8,128)(2,1)}), (bf16[256,2560]{1,0:T(8,128)(2,1)}, bf16[256,2048]{1,0:T(8,128)(2,1)}, ...) | async-done | bytes 11010064 | tf_op jit(solution)/shard_map/psum | solution.py:258
  (239 shorter events, 175.4 us)
Async XLA Ops:
  7.2 104.6 %all-gather.5.cloned.1.call-start = ((), (), s32[]{:S(2)}) async-start(), calls=%async_computation.12 | async-start | bytes 11796480 | tf_op jit(solution)/shard_map/all_gather | solution.py:46
  7.9 193.1 %all-gather.7.cloned.1.call-start = ((), (), s32[]{:S(2)}) async-start(), calls=%async_computation.13 | async-start | bytes 9437184 | tf_op jit(solution)/shard_map/all_gather | solution.py:46
  8.7 578.5 %all-gather.9.cloned.1.call-start = ((), (), s32[]{:S(2)}) async-start(), calls=%async_computation.14 | async-start | bytes 51904512 | tf_op jit(solution)/shard_map/all_gather | solution.py:46
  9.4 102.4 %copy-start.32 = (f32[2048]{0:T(1024)S(1)}, f32[2048]{0:T(1024)}, u32[]{:S(2)}) copy-start(f32[2048]{0:T(1024)} %param.18) | copy-start | bytes 24580
  9.4 780.2 %all-gather.11.cloned.1.call-start = ((), (), s32[]{:S(2)}) async-start(), calls=%async_computation.15 | async-start | bytes 25952256 | tf_op jit(solution)/shard_map/all_gather | solution.py:46
  10.8 100.9 %copy-start.36 = (f32[256]{0:T(256)}, f32[256]{0:T(256)S(1)}, u32[]{:S(2)}) copy-start(f32[256]{0:T(256)S(1)} %get-tuple-element.329) | copy-start | bytes 3076
  119.5 8.7 all-to-all-start.1
  123.1 20.2 copy-start.34
  128.1 8.3 all-to-all-start.2
  131.5 11.9 copy-start.39
  136.4 16.8 all-to-all-start
  142.2 16.7 copy-start.19
  196.9 16.7 all-to-all-start.3
  200.4 878.0 %reduce-scatter.9.cloned.1.call-start = ((), (), s32[]{:S(2)}) async-start(), calls=%async_computation.17 | async-start | bytes 9437184 | tf_op jit(solution)/shard_map/reduce_scatter | solution.py:61
  213.6 373.6 %copy-start.25 = (f32[2048]{0:T(1024)S(1)}, f32[2048]{0:T(1024)}, u32[]{:S(2)}) copy-start(f32[2048]{0:T(1024)} %param.21) | copy-start | bytes 24580
  221.8 608.4 %copy-start.27 = (f32[256]{0:T(256)}, f32[256]{0:T(256)S(1)}, u32[]{:S(2)}) copy-start(f32[256]{0:T(256)S(1)} %get-tuple-element.331) | copy-start | bytes 3076
  612.9 195.2 %copy-start.3 = (f32[256,2048]{1,0:T(8,128)S(1)}, f32[256,2048]{1,0:T(8,128)}, u32[]{:S(2)}) copy-start(f32[256,2048]{1,0:T(8,128)} %get-tuple-element.333) | copy-start | bytes 6291460
  848.8 17.8 all-to-all-start.4
  895.3 13.7 slice-start
  959.7 13.4 slice-start
  999.2 10.0 all-to-all-start.7
  1009.2 9.2 all-to-all-start.6
  1013.4 133.7 %reduce-scatter.7.cloned.1.call-start = ((), (), s32[]{:S(2)}) async-start(), calls=%async_computation.16 | async-start | bytes 11796480 | tf_op jit(solution)/shard_map/reduce_scatter | solution.py:61
  1013.5 20.7 %copy-start.2 = (bf16[1,256,2048]{2,1,0:T(8,128)(2,1)S(1)}, bf16[1,256,2048]{2,1,0:T(8,128)(2,1)}, u32[]{:S(2)}) copy-start(bf16[1,256,2048]{2,1,0:T(8,128)(2,1)} %param.14) | copy-start | bytes 3145732
  1013.5 20.7 %copy-start.33 = (f32[2048]{0:T(1024)S(1)}, f32[2048]{0:T(1024)}, u32[]{:S(2)}) copy-start(f32[2048]{0:T(1024)} %param.18) | copy-start | bytes 24580
  1013.5 20.7 %copy-start.37 = (f32[256]{0:T(256)S(1)}, f32[256]{0:T(256)}, u32[]{:S(2)}) copy-start(f32[256]{0:T(256)} %copy-done.36) | copy-start | bytes 3076
  1041.0 334.4 %reduce-scatter.11.cloned.1.call-start = ((), (), s32[]{:S(2)}) async-start(), calls=%async_computation.18 | async-start | bytes 25952256 | tf_op jit(solution)/shard_map/reduce_scatter | solution.py:61
  1055.4 764.5 %reduce-scatter.13.cloned.1.call-start = ((), (), s32[]{:S(2)}) async-start(), calls=%async_computation.19 | async-start | bytes 51904512
  1078.3 959.5 %all-reduce.5.cloned.1.call-start = ((), (), s32[]{:S(2)}) async-start(), calls=%async_computation.20 | async-start | bytes 22020096 | tf_op jit(solution)/shard_map/psum | solution.py:258
  1819.9 13.5 copy-start.17
  1833.4 47.8 %copy-start.7 = (f32[256,2048]{1,0:T(8,128)S(1)}, f32[256,2048]{1,0:T(8,128)}, u32[]{:S(2)}) copy-start(f32[256,2048]{1,0:T(8,128)} %copy-done.5) | copy-start | bytes 6291460
  1833.4 47.8 %copy-start.41 = (f32[256]{0:T(256)S(1)}, f32[256]{0:T(256)}, u32[]{:S(2)}) copy-start(f32[256]{0:T(256)} %get-tuple-element.328) | copy-start | bytes 3076
  (40 other events, 187.0 us)
Sparse Core Ops, SparseCore 0:
  9.6 102.0 all-gather.4
  113.3 80.3 all-gather.6
  195.4 391.6 all-gather.8
  588.6 200.9 all-gather.10
  839.9 87.6 reduce-scatter.8
  1041.1 106.0 reduce-scatter.6
  1149.5 225.8 reduce-scatter.10
  1377.7 442.1 reduce-scatter.12
  1823.8 213.9 all-reduce.4
where the time goes:
time: 2070 us; the launch traced here: 2060 us
  waiting for transfers between devices  1590 us (77%)
  matrix products  236 us (11%)
  local copies, waits for them, and re-layouts  77 us (4%)
  other arithmetic  58.8 us (3%)
  blocking collectives  53.5 us (3%)
  starting transfers between devices  28 us (1%)
    all_gather x4, waiting for transfers between devices, fold_product(): lax.all_gather(weight, 'batch', axis=0, tiled=True)  643 us
    unnamed x10, waiting for transfers between devices  447 us
    reduce_scatter x3, waiting for transfers between devices, weight_gradient(): lax.psum_scatter(lax.dot_general(inputs, grads_out, (((0,), (0,)), ((), (...  297 us
    psum x1, waiting for transfers between devices, local(): lax.psum(qkv_part.astype(jnp.bfloat16), 'seq').astype(jnp.float32)  153 us
    dot_general x4, matrix products, transposed_product(): lax.dot_general(grads_out, lax.all_gather(weight, 'batch', axis=0, tiled=...  56 us
    dot_general x4, matrix products, fold_product(): jnp.dot(inputs, lax.all_gather(weight, 'batch', axis=0, tiled=True), pref...  54.3 us
    dot_general x4, matrix products, weight_gradient(): lax.dot_general(inputs, grads_out, (((0,), (0,)), ((), ())), preferred_el...  47 us
  transfers between devices with their start and end apart: 16, of which 13 were waited for; matrix products, arithmetic and copies ran while one was open for 15% of the time, Pallas kernels for 0%

commit v1 on v0

--- a/solution.py
+++ b/solution.py
@@ -255,7 +255,7 @@
     )
     attn_gain_grad, mlp_gain_grad = lax.psum((attn_term, mlp_term), ("seq", "batch"))
     qkv_grad, out_grad, gate_up_grad, down_grad = (
-        lax.psum(qkv_part.astype(jnp.bfloat16), "seq").astype(jnp.float32),
+        jnp.sum(lax.all_gather(qkv_part.astype(jnp.bfloat16), "seq"), axis=0).astype(jnp.float32),
         lax.psum(out_part.astype(jnp.bfloat16), "seq").astype(jnp.float32),
         lax.psum(gate_up_part.astype(jnp.bfloat16), "seq").astype(jnp.float32),
         lax.psum(down_part.astype(jnp.bfloat16), "seq").astype(jnp.float32),

time: 2070 us -> 2190 us (1.058)
  waiting for transfers between devices: 1590 us -> 1710 us
    reduce_scatter x3, waiting for transfers between devices: 297 us -> 378 us  [weight_gradient(): lax.psum_scatter(lax.dot_general(inputs, grads_out, (((0,), (0,)), ((), (...]
    psum x1, waiting for transfers between devices: 153 us -> 190 us  [local(): lax.psum(out_part.astype(jnp.bfloat16), 'seq').astype(jnp.float32)]
    unnamed x10 -> x11, waiting for transfers between devices: 447 us -> 447 us
  transfers between devices with their start and end apart: 16 -> 17, of which waited for: 13 -> 14; matrix products, arithmetic and copies ran while one was open for 15% -> 8% of each run, Pallas kernels for 0% -> 0%
where the time goes in v1:
time: 2190 us; the launch traced here: 2180 us
  waiting for transfers between devices  1710 us (78%)
  matrix products  236 us (11%)
  local copies, waits for them, and re-layouts  78 us (4%)
  other arithmetic  65.9 us (3%)
  blocking collectives  53.3 us (2%)
  starting transfers between devices  27.3 us (1%)
    all_gather x4, waiting for transfers between devices, fold_product(): lax.all_gather(weight, 'batch', axis=0, tiled=True)  642 us
    unnamed x11, waiting for transfers between devices  447 us
    reduce_scatter x3, waiting for transfers between devices, weight_gradient(): lax.psum_scatter(lax.dot_general(inputs, grads_out, (((0,), (0,)), ((), (...  378 us
    psum x1, waiting for transfers between devices, local(): lax.psum(out_part.astype(jnp.bfloat16), 'seq').astype(jnp.float32)  190 us
    dot_general x4, matrix products, transposed_product(): lax.dot_general(grads_out, lax.all_gather(weight, 'batch', axis=0, tiled=...  55.6 us
    dot_general x4, matrix products, fold_product(): jnp.dot(inputs, lax.all_gather(weight, 'batch', axis=0, tiled=True), pref...  54 us
    dot_general x4, matrix products, weight_gradient(): lax.dot_general(inputs, grads_out, (((0,), (0,)), ((), ())), preferred_el...  48.4 us
  transfers between devices with their start and end apart: 17, of which 14 were waited for; matrix products, arithmetic and copies ran while one was open for 8% of the time, Pallas kernels for 0%

profile of v1, /device:TPU:0, one launch (start us, length us, event | category | flops | bytes accessed | tf_op | source)
XLA Modules:
  0.0 2184.9 jit_solution(6934688901191031560)
XLA Ops:
  10.9 100.9 %all-gather.7.cloned.1.call-done = bf16[2048,2560]{1,0:T(8,128)(2,1)} async-done(((bf16[256,2560]{1,0:T(8,128)(2,1)}), bf16[2048,2560]{1,0:T(8,128)(2,1)}) %all-gather.7.cloned.1.call-update) | async-done | bytes 10485776 | tf_op jit(solution)/shard_map/all_gather | solution.py:46
  144.6 8.7 all-to-all-done
  159.6 31.4 %while.29 = (s32[]{:T(128)}, bf16[2,512,1,8,64]{1,4,3,2,0:T(8,128)(2,1)}, f32[2,1,8,512]{3,2,1,0:T(8,128)}, s32[1024]{0:T(1024)S(1)}, s32[2]{0:T(128)S(1)}, /*in...) while((s32[]{:T(128)}, ...), condition=%wide.region_4.5_spmd.clone, body=%wide.region_1.4_spmd.clone.sunk | while | flops 1121710080 | bytes 63066468 | solution.py:156
  201.0 13.1 all-to-all-done.3
  214.1 8.1 multiply_reduce_fusion.2
  222.3 364.9 %all-gather.11.cloned.1.call-done = bf16[2048,11264]{1,0:T(8,128)(2,1)} async-done(((bf16[256,11264]{1,0:T(8,128)(2,1)}), bf16[2048,11264]{1,0:T(8,128)(2,1)}) %all-gather.11.cloned.1.call-update) | async-done | bytes 46137360 | tf_op jit(solution)/shard_map/all_gather | solution.py:46
  587.1 25.7 %fusion.103 = f32[256,11264]{1,0:T(8,128)} fusion(bf16[2048,11264]{1,0:T(8,128)(2,1)} %all-gather.11.cloned.1.call-done, f32[256,2048]{1,0:T(8,128)} %get-tuple-element.332, f32[2048]{0:T(1024)S(1)} %copy-done.21, f32[256]{0:T(256)S(1)} %get-tuple-element.330), kind=kOutput, calls=%fused_computation.150 | convolution fusion | flops 11812732928 | bytes 59778048 | tf_op jit(solution)/shard_map/dot_general | solution.py:44
  612.9 176.7 %all-gather.13.cloned.1.call-done = bf16[5632,2048]{1,0:T(8,128)(2,1)} async-done(((bf16[704,2048]{1,0:T(8,128)(2,1)}), bf16[5632,2048]{1,0:T(8,128)(2,1)}) %all-gather.13.cloned.1.call-update) | async-done | bytes 23068688 | tf_op jit(solution)/shard_map/all_gather | solution.py:46
  789.6 18.5 multiply_convert_fusion.1
  808.1 22.1 %multiply_reduce_fusion = (f32[2048]{0:T(1024)}, f32[256]{0:T(256)S(1)}, f32[256,2048]{1,0:T(8,128)}) fusion(f32[256,2048]{1,0:T(8,128)S(1)} %copy-done.3, f32[256]{0:T(256)S(1)} %get-tuple-element.330, f32[2048]{0:T(1024)S(1)} %copy-done.21, bf16[2048,11264]{1,0:T(8,128)(2,1)} %all-gather.11.cloned.1.call-done, bf16[256,5632]{1,0:T(8,128)(2,1)} %get-tuple-element.312, ...), kind=kOutput, calls=%fused_computation.91 | convolution fusion | flops 11825838080 | bytes 56117248 | tf_op jit(solution)/shard_map/dot_general | solution.py:52
  843.9 14.2 all-to-all-done.4
  860.9 129.5 %while.30 = (s32[]{:T(128)}, f32[1024,1,64]{0,2,1:T(8,128)}, f32[1024,1,64]{0,2,1:T(8,128)}, f32[2,512,1,8,64]{1,0,4,3,2:T(2,128)}, s32[2]{0:T(128)}, /*index=5*...) while((s32[]{:T(128)}, f32[1024,1,64]{0,2,1:T(8,128)}, ...), condition=%wide.region_9.10_spmd.clone.clone, body=%wide.region_7.9_spmd.clone.clone.sunk | while | flops 2724261888 | bytes 167350704 | solution.py:218
  868.4 10.3 fusion.150
  878.7 9.3 fusion.151
  893.9 7.5 fusion.153
  906.2 19.5 dynamic_update_slice.23
  933.1 10.3 fusion.150
  943.4 9.3 fusion.151
  958.6 7.6 fusion.153
  970.9 19.5 dynamic_update_slice.23
  1011.8 14.5 all_to_all.125
  1043.9 12.9 convolution_convert_fusion.1
  1058.4 21.7 convolution_convert_fusion
  1080.2 60.1 %reduce-scatter.7.cloned.1.call-done = bf16[256,2560]{1,0:T(8,128)(2,1)} async-done(((bf16[2048,2560]{1,0:T(8,128)(2,1)}), bf16[256,2560]{1,0:T(8,128)(2,1)}) %reduce-scatter.7.cloned.1.call-update) | async-done | bytes 1310736 | tf_op jit(solution)/shard_map/reduce_scatter | solution.py:61
  1140.4 90.1 %reduce-scatter.9.cloned.1.call-done = bf16[256,2048]{1,0:T(8,128)(2,1)} async-done(((bf16[2048,2048]{1,0:T(8,128)(2,1)}), bf16[256,2048]{1,0:T(8,128)(2,1)}) %reduce-scatter.9.cloned.1.call-update) | async-done | bytes 1048592 | tf_op jit(solution)/shard_map/reduce_scatter | solution.py:61
  1230.5 228.2 %reduce-scatter.11.cloned.1.call-done = bf16[704,2048]{1,0:T(8,128)(2,1)} async-done(((bf16[5632,2048]{1,0:T(8,128)(2,1)}), bf16[704,2048]{1,0:T(8,128)(2,1)}) %reduce-scatter.11.cloned.1.call-update) | async-done | bytes 2883600 | tf_op jit(solution)/shard_map/reduce_scatter | solution.py:61
  1458.7 444.5 %reduce-scatter.13.cloned.1.call-done = bf16[256,11264]{1,0:T(8,128)(2,1)} async-done(((bf16[2048,11264]{1,0:T(8,128)(2,1)}), bf16[256,11264]{1,0:T(8,128)(2,1)}) %reduce-scatter.13.cloned.1.call-update) | async-done | bytes 5767184
  1903.2 13.2 fusion.59
  1916.5 8.6 fusion.69
  1925.0 38.8 %all-reduce.1 = (f32[2048]{0:T(1024)}, f32[2048]{0:T(1024)}) all-reduce(f32[2048]{0:T(1024)S(1)} %get-tuple-element.252, f32[2048]{0:T(1024)S(1)} %copy-done.37), channel_id=1, replica_groups=mesh['seq'=4,'batch'=8] {'seq','batch'}, use_global_device_ids=true, to_apply=%region_12.13 | all-reduce | flops 4096 | bytes 32768 | tf_op jit(solution)/shard_map/psum | solution.py:256
  1972.8 190.4 %all-reduce.5.cloned.1.call-done = (bf16[256,2048]{1,0:T(8,128)(2,1)}, bf16[256,11264]{1,0:T(8,128)(2,1)}, bf16[704,2048]{1,0:T(8,128)(2,1)}) async-done(((bf16[256,2048]{1,0:T(8,128)(2,1)}, bf16[256,11264]{1,0:T(8,128)(2,1)}, bf16[704,2048]{1,0:T(8,128)(2,1)}), (bf16[256,2048]{1,0:T(8,128)(2,1)}, bf16[256,11264]{1,0:T(8,128)(2,1)}, bf16[704,2048]{1,0:T(8,128)(2,1)})) %all-reduce.5.cloned.1.call-update) | async-done | bytes 9699344 | tf_op jit(solution)/shard_map/psum | solution.py:259
  2166.0 8.6 convert_element_type.195
  (239 shorter events, 189.2 us)
Async XLA Ops:
  7.2 104.6 %all-gather.7.cloned.1.call-start = ((), (), s32[]{:S(2)}) async-start(), calls=%async_computation.12 | async-start | bytes 11796480 | tf_op jit(solution)/shard_map/all_gather | solution.py:46
  7.9 193.1 %all-gather.9.cloned.1.call-start = ((), (), s32[]{:S(2)}) async-start(), calls=%async_computation.13 | async-start | bytes 9437184 | tf_op jit(solution)/shard_map/all_gather | solution.py:46
  8.7 578.5 %all-gather.11.cloned.1.call-start = ((), (), s32[]{:S(2)}) async-start(), calls=%async_computation.14 | async-start | bytes 51904512 | tf_op jit(solution)/shard_map/all_gather | solution.py:46
  9.4 102.4 %copy-start.31 = (f32[2048]{0:T(1024)S(1)}, f32[2048]{0:T(1024)}, u32[]{:S(2)}) copy-start(f32[2048]{0:T(1024)} %param.18) | copy-start | bytes 24580
  9.4 780.2 %all-gather.13.cloned.1.call-start = ((), (), s32[]{:S(2)}) async-start(), calls=%async_computation.15 | async-start | bytes 25952256 | tf_op jit(solution)/shard_map/all_gather | solution.py:46
  10.9 100.9 %copy-start.35 = (f32[256]{0:T(256)}, f32[256]{0:T(256)S(1)}, u32[]{:S(2)}) copy-start(f32[256]{0:T(256)S(1)} %get-tuple-element.328) | copy-start | bytes 3076
  119.5 8.7 all-to-all-start.1
  123.1 20.2 copy-start.33
  128.1 8.3 all-to-all-start.2
  136.4 16.8 all-to-all-start
  142.2 16.7 copy-start.16
  196.9 17.2 all-to-all-start.3
  214.1 373.0 %copy-start.21 = (f32[2048]{0:T(1024)S(1)}, f32[2048]{0:T(1024)}, u32[]{:S(2)}) copy-start(f32[2048]{0:T(1024)} %param.21) | copy-start | bytes 24580
  222.3 607.9 %copy-start.24 = (f32[256]{0:T(256)}, f32[256]{0:T(256)S(1)}, u32[]{:S(2)}) copy-start(f32[256]{0:T(256)S(1)} %get-tuple-element.330) | copy-start | bytes 3076
  612.9 195.3 %copy-start.3 = (f32[256,2048]{1,0:T(8,128)S(1)}, f32[256,2048]{1,0:T(8,128)}, u32[]{:S(2)}) copy-start(f32[256,2048]{1,0:T(8,128)} %get-tuple-element.332) | copy-start | bytes 6291460
  840.3 17.8 all-to-all-start.4
  860.9 134.8 %copy-start.34 = (f32[1,1024]{1,0:T(1,128)S(1)}, f32[1,1024]{1,0:T(1,128)}, u32[]{:S(2)}) copy-start(f32[1,1024]{1,0:T(1,128)} %copy-done.33) | copy-start | bytes 12292
  888.0 13.4 slice-start
  952.7 13.4 slice-start
  992.2 10.4 all-to-all-start.7
  1002.7 9.2 all-to-all-start.6
  1006.8 133.5 %reduce-scatter.7.cloned.1.call-start = ((), (), s32[]{:S(2)}) async-start(), calls=%async_computation.16 | async-start | bytes 11796480 | tf_op jit(solution)/shard_map/reduce_scatter | solution.py:61
  1006.9 20.4 copy-start.2
  1006.9 20.4 copy-start.32
  1006.9 20.4 copy-start.36
  1034.1 196.4 %reduce-scatter.9.cloned.1.call-start = ((), (), s32[]{:S(2)}) async-start(), calls=%async_computation.17 | async-start | bytes 9437184 | tf_op jit(solution)/shard_map/reduce_scatter | solution.py:61
  1042.7 416.0 %reduce-scatter.11.cloned.1.call-start = ((), (), s32[]{:S(2)}) async-start(), calls=%async_computation.18 | async-start | bytes 25952256 | tf_op jit(solution)/shard_map/reduce_scatter | solution.py:61
  1056.8 846.4 %reduce-scatter.13.cloned.1.call-start = ((), (), s32[]{:S(2)}) async-start(), calls=%async_computation.20 | async-start | bytes 51904512
  1080.2 886.8 %all-gather.15.cloned.1.call-start = ((), (), s32[]{:S(2)}) async-start(), calls=%async_computation.19 | async-start | bytes 6553600 | tf_op jit(solution)/shard_map/all_gather | solution.py:258
  1140.3 1022.9 %all-reduce.5.cloned.1.call-start = ((), (), s32[]{:S(2)}) async-start(), calls=%async_computation.21 | async-start | bytes 19398656 | tf_op jit(solution)/shard_map/psum | solution.py:259
  1916.4 47.4 %copy-start.7 = (f32[256,2048]{1,0:T(8,128)S(1)}, f32[256,2048]{1,0:T(8,128)}, u32[]{:S(2)}) copy-start(f32[256,2048]{1,0:T(8,128)} %copy-done.5) | copy-start | bytes 6291460
  1916.5 47.4 %copy-start.39 = (f32[256]{0:T(256)S(1)}, f32[256]{0:T(256)}, u32[]{:S(2)}) copy-start(f32[256]{0:T(256)} %get-tuple-element.327) | copy-start | bytes 3076
  (39 other events, 192.5 us)
Sparse Core Ops, SparseCore 0:
  9.6 102.0 all-gather.6
  113.3 80.3 all-gather.8
  195.4 391.6 all-gather.10
  588.6 200.9 all-gather.12
  1034.2 106.0 reduce-scatter.6
  1142.5 87.9 reduce-scatter.8
  1232.8 225.7 reduce-scatter.10
  1461.0 442.1 reduce-scatter.12
  1905.0 60.9 all-gather.14
  1969.8 193.3 all-reduce.4
